TPU v7x, 32 devices: a whole 2x2x4 slice. The times are simulated.
32 devices in a mesh: groups: 2 (over y), frame: 4 (over z), strip: 2 (over x), slab: 2 (over core).
Axes of the slice: x: 2, y: 2, z: 4, core: 2. Of those that a mesh axis runs over, the one named last changes fastest.
Arguments:
- frames_in: bfloat16 [16, 8, 128, 192], P(('groups', 'frame'), 'strip', 'slab'), parts along dimension 0, may hold values from -6 to 6
- weight_first: bfloat16 [3, 3, 3, 192, 192], replicated, may hold values from -0.078125 to 0.078125
- scale_first: float32 [192], replicated, may hold values from 0.25 to 1.75
- weight_second: bfloat16 [3, 3, 3, 192, 192], replicated, may hold values from -0.078125 to 0.078125
- scale_second: float32 [192], replicated, may hold values from 0.25 to 1.75
Outputs:
- latents_out: bfloat16 [16, 8, 128, 192], P(('groups', 'frame'), 'strip', 'slab'), parts along dimension 0
There are 2 independent parts, one for each index of `groups`. A program takes and returns all parts, laid end to end along the dimension named above; an argument that names none is the same for every part. Nothing has to cross between parts.
All inputs are finite; a program needn't handle non-finite values.
Results may differ from a plain program's by a relative error of at most 0.0051.
Values may be sent and summed in bfloat16 or wider, within the bound.
A program may use at most 64 MiB of HBM per device.

v0:
```python
import jax
import jax.numpy as jnp
from jax import lax
from jax.sharding import PartitionSpec as P


def from_behind(x, axis, by):
    size = lax.axis_size(axis)
    pairs = [(i, i + by) for i in range(size) if 0 <= i + by < size]
    return lax.ppermute(x, axis, pairs)


def with_halo(cells, sides, width):
    for axis, dim in sides:
        count = lax.axis_size(axis)
        ends = count - 1
        head = lax.slice_in_dim(cells, 0, width, axis=dim)
        tail = lax.slice_in_dim(cells, cells.shape[dim] - width, cells.shape[dim], axis=dim)
        cells = jnp.concatenate(
            [
                lax.ppermute(tail, axis, [(i, (i + 1) % count) for i in range(ends)]),
                cells,
                lax.ppermute(head, axis, [((i + 1) % count, i) for i in range(ends)]),
            ],
            axis=dim,
        )
    return cells


def tap_block(block, rows, cols):
    count = block.shape[0]
    pieces = [
        block[:, offset_y : offset_y + rows, offset_x : offset_x + cols]
        for offset_y in range(3)
        for offset_x in range(3)
    ]
    return jnp.concatenate(pieces, axis=-1).reshape(count * rows * cols, -1)


def finish(convolved, scales):
    mean_square = jnp.mean(convolved * convolved, axis=-1, keepdims=True)
    normed = convolved * lax.rsqrt(mean_square + 1e-06) * scales
    return jax.nn.silu(normed).astype(jnp.bfloat16)


def conv_layer(features, weight, scales):
    frames, rows, cols, channels = features.shape
    flat_weight = weight.reshape(3, 9 * channels, channels)
    cells = rows * cols
    earlier = from_behind(features, "frame", 1)
    extended = jnp.concatenate([earlier, features], axis=0)
    padded = with_halo(extended, (("strip", 1), ("slab", 2)), 1)
    accumulated = jnp.zeros((frames * cells, channels), jnp.float32)
    for offset_t in range(3):
        accumulated = accumulated + jnp.dot(
            tap_block(padded[offset_t : offset_t + frames], rows, cols),
            flat_weight[offset_t],
            preferred_element_type=jnp.float32,
        )
    accumulated = accumulated.reshape(frames, cells, channels)
    return finish(accumulated, scales).reshape(frames, rows, cols, channels)


def shards(frames_in, weight_first, scale_first, weight_second, scale_second):
    hidden = conv_layer(frames_in, weight_first, scale_first)
    return conv_layer(hidden, weight_second, scale_second)


def solution(mesh):
    return jax.shard_map(
        shards,
        mesh=mesh,
        in_specs=(P(("groups", "frame"), "strip", "slab", None), P(), P(), P(), P()),
        out_specs=P(("groups", "frame"), "strip", "slab", None),
        check_vma=False,
    )
```

profile of v0, /device:TPU:0, one launch (start us, length us, event | category | flops | bytes accessed | tf_op | source)
XLA Modules:
  0.0 92.0 jit_solution(4176239762942542063)
XLA Ops:
  0.0 5.0 %collective-permute-start = (bf16[2,4,64,192]{3,2,1,0:T(8,128)(2,1)}, bf16[2,4,64,192]{3,2,1,0:T(8,128)(2,1)S(1)}, u32[]{:S(2)}, u32[]{:S(2)}) collective-permute-start(bf16[2,4,64,192]{3,2,1,0:T(8,128)(2,1)} %param.5), channel_id=1, source_target_pairs={{0,4},{4,8},{8,12},{1,5},{5,9},{9,13},{2,6},{6,10},{10,14},{3,7},{... | collective-permute-start | bytes 589832 | tf_op jit(solution)/shard_map/ppermute | solution.py:10
  5.0 5.8 %collective-permute-done = bf16[2,4,64,192]{3,2,1,0:T(8,128)(2,1)S(1)} collective-permute-done((bf16[2,4,64,192]{3,2,1,0:T(8,128)(2,1)}, bf16[2,4,64,192]{3,2,1,0:T(8,128)(2,1)S(1)}, u32[]{:S(2)}, u32[]{:S(2)}) %collective-permute-start) | collective-permute-done | bytes 196640 | tf_op jit(solution)/shard_map/ppermute | solution.py:10
  10.8 0.0 copy-start.2
  10.8 1.1 %constant_dynamic-update-slice_fusion = bf16[4,4,64,192]{3,2,1,0:T(8,128)(2,1)S(1)} fusion(bf16[4,4,64,192]{3,2,1,0:T(8,128)(2,1)S(1)} %constant_dynamic-update-slice_fusion.1, bf16[2,4,64,192]{3,2,1,0:T(8,128)(2,1)} %param.5), kind=kLoop, calls=%fused_computation.38 | loop fusion | bytes 458752 | tf_op jit(solution)/shard_map/concatenate | solution.py:51
  11.9 3.4 %collective-permute-start.1 = (bf16[4,1,64,192]{3,2,1,0:T(8,128)(2,1)S(1)}, bf16[4,1,64,192]{3,2,1,0:T(8,128)(2,1)S(1)}, u32[]{:S(2)}, u32[]{:S(2)}) collective-permute-start(bf16[4,1,64,192]{3,2,1,0:T(8,128)(2,1)S(1)} %get-tuple-element.75), channel_id=1, source_target_pairs={{0,2},{1,3},{4,6},{5,7},{8,10},{9,11},{12,14},{13,15},{16,18},{17,... | collective-permute-start | bytes 294920 | tf_op jit(solution)/shard_map/ppermute | solution.py:21
  15.3 0.0 copy-done.2
  15.4 1.3 %collective-permute-start.2 = (bf16[4,1,64,192]{3,2,1,0:T(8,128)(2,1)S(1)}, bf16[4,1,64,192]{3,2,1,0:T(8,128)(2,1)S(1)}, u32[]{:S(2)}, u32[]{:S(2)}) collective-permute-start(bf16[4,1,64,192]{3,2,1,0:T(8,128)(2,1)S(1)} %get-tuple-element.76), channel_id=1, source_target_pairs={{2,0},{3,1},{6,4},{7,5},{10,8},{11,9},{14,12},{15,13},{18,16},{19,... | collective-permute-start | bytes 294920 | tf_op jit(solution)/shard_map/ppermute | solution.py:23
  16.7 3.2 %fusion.7 = (bf16[1,3,3,192,192]{4,3,2,1,0:T(8,128)(2,1)S(1)}, bf16[1,3,3,192,192]{4,3,2,1,0:T(8,128)(2,1)}, bf16[1,3,3,192,192]{4,3,2,1,0:T(8,128)(2,1)}) fusion(bf16[3,3,3,192,192]{4,3,2,1,0:T(8,128)(2,1)} %param.6), kind=kLoop, calls=%fused_computation.43 | loop fusion | bytes 3981312 | tf_op jit(solution)/shard_map/slice | solution.py:57
  19.8 0.0 collective-permute-done.1
  19.8 2.4 %collective-permute-done.2 = bf16[4,1,64,192]{3,2,1,0:T(8,128)(2,1)S(1)} collective-permute-done((bf16[4,1,64,192]{3,2,1,0:T(8,128)(2,1)S(1)}, bf16[4,1,64,192]{3,2,1,0:T(8,128)(2,1)S(1)}, u32[]{:S(2)}, u32[]{:S(2)}) %collective-permute-start.2) | collective-permute-done | bytes 98336 | tf_op jit(solution)/shard_map/ppermute | solution.py:23
  22.3 1.3 %collective-permute-start.3 = (bf16[4,6,1,192]{3,2,1,0:T(2,128)(2,1)S(1)}, bf16[4,6,1,192]{3,2,1,0:T(2,128)(2,1)S(1)}, u32[]{:S(2)}, u32[]{:S(2)}) collective-permute-start(bf16[4,6,1,192]{3,2,1,0:T(2,128)(2,1)S(1)} %get-tuple-element.54), channel_id=1, source_target_pairs={{0,1},{2,3},{4,5},{6,7},{8,9},{10,11},{12,13},{14,15},{16,17},{18,... | collective-permute-start | bytes 27656 | tf_op jit(solution)/shard_map/ppermute | solution.py:21
  23.6 1.3 %collective-permute-start.4 = (bf16[4,6,1,192]{3,2,1,0:T(2,128)(2,1)S(1)}, bf16[4,6,1,192]{3,2,1,0:T(2,128)(2,1)S(1)}, u32[]{:S(2)}, u32[]{:S(2)}) collective-permute-start(bf16[4,6,1,192]{3,2,1,0:T(2,128)(2,1)S(1)} %get-tuple-element.53), channel_id=1, source_target_pairs={{1,0},{3,2},{5,4},{7,6},{9,8},{11,10},{13,12},{15,14},{17,16},{19,... | collective-permute-start | bytes 27656 | tf_op jit(solution)/shard_map/ppermute | solution.py:23
  24.9 1.3 %fusion.3 = (bf16[2,4,64,192]{3,2,1,0:T(8,128)(2,1)}, bf16[2,4,64,192]{3,2,1,0:T(8,128)(2,1)}, bf16[2,4,64,192]{3,2,1,0:T(8,128)(2,1)}, bf16[2,4,64,192]{3,2,1,0...) fusion(bf16[4,4,64,192]{3,2,1,0:T(8,128)(2,1)S(1)} %constant_dy, ...), kind=kLoop, calls=%fused_computation.23 | loop fusion | flops 589824 | bytes 2424832 | tf_op jit(solution)/shard_map/concatenate | solution.py:19
  26.2 0.0 collective-permute-done.3
  26.2 0.5 collective-permute-done.4
  26.7 0.5 pad_maximum_fusion
  27.1 2.1 %fusion.10 = (bf16[2,4,64,192]{3,2,1,0:T(8,128)(2,1)}, bf16[2,4,64,192]{3,2,1,0:T(8,128)(2,1)S(1)}, bf16[2,4,64,192]{3,2,1,0:T(8,128)(2,1)}, bf16[2,4,64,192]{3,...) fusion(bf16[4,6,65,192]{3,2,1,0:T(8,128)(2,1)S(1)} %get-tuple-e, ...), kind=kLoop, calls=%fused_computation.46 | loop fusion | bytes 7077888 | tf_op jit(solution)/shard_map/slice | solution.py:33
  29.2 2.8 %concatenate.103 = bf16[2,4,64,1728]{3,2,1,0:T(8,128)(2,1)S(1)} concatenate(bf16[2,4,64,192]{3,2,1,0:T(8,128)(2,1)} %get-tuple-element.83, bf16[2,4,64,192]{3,2,1,0:T(8,128)(2,1)} %get-tuple-element.71, bf16[2,4,64,192]{3,2,1,0:T(8,128)(2,1)} %get-tuple-element.35, bf16[2,4,64,192]{3,2,1,0:T(8,128)(2,1)} %get-tuple-element.84, bf16[2,4,64,192]{3,2,1,0:T(8,128)(2,1)} %get-tuple-element.74, ...), dimensions={3} | concatenate | bytes 3538944 | tf_op jit(solution)/shard_map/concatenate | solution.py:37
  32.0 1.9 %fusion.15 = f32[512,192]{0,1:T(8,128)S(1)} fusion(bf16[512,1728]{1,0:T(8,128)(2,1)S(1)} %bitcast.28, bf16[1728,192]{1,0:T(8,128)(2,1)} %bitcast.37), kind=kOutput, calls=%fused_computation.51 | convolution fusion | flops 339738624 | bytes 2826240 | tf_op jit(solution)/shard_map/dot_general | solution.py:55
  33.9 2.8 %concatenate.104 = bf16[2,4,64,1728]{3,2,1,0:T(8,128)(2,1)S(1)} concatenate(bf16[2,4,64,192]{3,2,1,0:T(8,128)(2,1)} %get-tuple-element.86, bf16[2,4,64,192]{3,2,1,0:T(8,128)(2,1)} %get-tuple-element.72, bf16[2,4,64,192]{3,2,1,0:T(8,128)(2,1)} %get-tuple-element.32, bf16[2,4,64,192]{3,2,1,0:T(8,128)(2,1)} %get-tuple-element.87, bf16[2,4,64,192]{3,2,1,0:T(8,128)(2,1)} %param.5, ...), dimensions={3} | concatenate | bytes 3538944 | tf_op jit(solution)/shard_map/concatenate | solution.py:37
  36.7 1.9 %fusion.16 = f32[512,192]{0,1:T(8,128)S(1)} fusion(bf16[512,1728]{1,0:T(8,128)(2,1)S(1)} %bitcast.31, bf16[1728,192]{1,0:T(8,128)(2,1)} %bitcast.36), kind=kOutput, calls=%fused_computation.52 | convolution fusion | flops 339738624 | bytes 2826240 | tf_op jit(solution)/shard_map/dot_general | solution.py:55
  38.7 2.9 %concatenate.102 = bf16[2,4,64,1728]{3,2,1,0:T(8,128)(2,1)S(1)} concatenate(bf16[2,4,64,192]{3,2,1,0:T(8,128)(2,1)} %get-tuple-element.81, bf16[2,4,64,192]{3,2,1,0:T(8,128)(2,1)} %get-tuple-element.73, bf16[2,4,64,192]{3,2,1,0:T(8,128)(2,1)} %get-tuple-element.37, bf16[2,4,64,192]{3,2,1,0:T(8,128)(2,1)} %get-tuple-element.82, bf16[2,4,64,192]{3,2,1,0:T(8,128)(2,1)} %copy-done.2, ...), dimensions={3} | concatenate | bytes 3538944 | tf_op jit(solution)/shard_map/concatenate | solution.py:37
  41.5 0.0 copy-start.3
  41.5 1.5 %multiply_reduce_fusion.1 = (f32[512]{0:T(512)S(1)}, f32[512,192]{0,1:T(8,128)}) fusion(f32[512,192]{0,1:T(8,128)S(1)} %fusion.16, f32[512,192]{0,1:T(8,128)S(1)} %fusion.15, bf16[512,1728]{1,0:T(8,128)(2,1)S(1)} %bitcast.26, bf16[1728,192]{1,0:T(8,128)(2,1)S(1)} %bitcast.34), kind=kOutput, calls=%fused_computation.21 | convolution fusion | flops 340131328 | bytes 3614720 | tf_op jit(solution)/shard_map/dot_general | solution.py:55
  43.1 1.2 %copy.8 = f32[512,192]{1,0:T(8,128)S(1)} copy(f32[512,192]{0,1:T(8,128)} %get-tuple-element.78) | data formatting | bytes 786432 | tf_op jit(solution)/shard_map/add | solution.py:55
  44.3 0.1 rsqrt.23
  44.3 0.0 copy-done.3
  44.4 0.2 multiply_convert_fusion.1
  44.6 4.3 %collective-permute-start.5 = (bf16[2,4,64,192]{3,2,1,0:T(8,128)(2,1)S(1)}, bf16[2,4,64,192]{3,2,1,0:T(8,128)(2,1)S(1)}, u32[]{:S(2)}, u32[]{:S(2)}) collective-permute-start(bf16[2,4,64,192]{3,2,1,0:T(8,128)(2,1)S(1)} %multiply_convert_fusion.1), channel_id=1, source_target_pairs={{0,4},{4,8},{8,12},{1,5},{5,9},{9,13},{2,6},{6,10},{10,14},{3,7},{... | collective-permute-start | bytes 589832 | tf_op jit(solution)/shard_map/ppermute | solution.py:10
  48.9 3.2 %fusion.6 = (bf16[1,3,3,192,192]{4,3,2,1,0:T(8,128)(2,1)S(1)}, bf16[1,3,3,192,192]{4,3,2,1,0:T(8,128)(2,1)}, bf16[1,3,3,192,192]{4,3,2,1,0:T(8,128)(2,1)}) fusion(bf16[3,3,3,192,192]{4,3,2,1,0:T(8,128)(2,1)} %param.8), kind=kLoop, calls=%fused_computation.42 | loop fusion | bytes 3981312 | tf_op jit(solution)/shard_map/slice | solution.py:57
  52.0 3.2 %collective-permute-done.5 = bf16[2,4,64,192]{3,2,1,0:T(8,128)(2,1)S(1)} collective-permute-done((bf16[2,4,64,192]{3,2,1,0:T(8,128)(2,1)S(1)}, bf16[2,4,64,192]{3,2,1,0:T(8,128)(2,1)S(1)}, u32[]{:S(2)}, u32[]{:S(2)}) %collective-permute-start.5) | collective-permute-done | bytes 196640 | tf_op jit(solution)/shard_map/ppermute | solution.py:10
  55.3 2.2 %collective-permute-start.6 = (bf16[4,1,64,192]{3,2,1,0:T(8,128)(2,1)S(1)}, bf16[4,1,64,192]{3,2,1,0:T(8,128)(2,1)S(1)}, u32[]{:S(2)}, u32[]{:S(2)}) collective-permute-start(bf16[4,1,64,192]{3,2,1,0:T(8,128)(2,1)S(1)} %get-tuple-element.69), channel_id=1, source_target_pairs={{0,2},{1,3},{4,6},{5,7},{8,10},{9,11},{12,14},{13,15},{16,18},{17,... | collective-permute-start | bytes 294920 | tf_op jit(solution)/shard_map/ppermute | solution.py:21
  57.5 1.3 %collective-permute-start.7 = (bf16[4,1,64,192]{3,2,1,0:T(8,128)(2,1)S(1)}, bf16[4,1,64,192]{3,2,1,0:T(8,128)(2,1)S(1)}, u32[]{:S(2)}, u32[]{:S(2)}) collective-permute-start(bf16[4,1,64,192]{3,2,1,0:T(8,128)(2,1)S(1)} %get-tuple-element.70), channel_id=1, source_target_pairs={{2,0},{3,1},{6,4},{7,5},{10,8},{11,9},{14,12},{15,13},{18,16},{19,... | collective-permute-start | bytes 294920 | tf_op jit(solution)/shard_map/ppermute | solution.py:23
  58.8 1.4 %collective-permute-done.6 = bf16[4,1,64,192]{3,2,1,0:T(8,128)(2,1)S(1)} collective-permute-done((bf16[4,1,64,192]{3,2,1,0:T(8,128)(2,1)S(1)}, bf16[4,1,64,192]{3,2,1,0:T(8,128)(2,1)S(1)}, u32[]{:S(2)}, u32[]{:S(2)}) %collective-permute-start.6) | collective-permute-done | bytes 98336 | tf_op jit(solution)/shard_map/ppermute | solution.py:21
  60.2 4.2 %collective-permute-done.7 = bf16[4,1,64,192]{3,2,1,0:T(8,128)(2,1)S(1)} collective-permute-done((bf16[4,1,64,192]{3,2,1,0:T(8,128)(2,1)S(1)}, bf16[4,1,64,192]{3,2,1,0:T(8,128)(2,1)S(1)}, u32[]{:S(2)}, u32[]{:S(2)}) %collective-permute-start.7) | collective-permute-done | bytes 98336 | tf_op jit(solution)/shard_map/ppermute | solution.py:23
  64.4 0.2 pad_maximum_fusion.2
  64.6 0.9 %fusion.12 = (bf16[2,4,64,192]{3,2,1,0:T(8,128)(2,1)}, bf16[2,4,64,192]{3,2,1,0:T(8,128)(2,1)}, bf16[2,4,64,192]{3,2,1,0:T(8,128)(2,1)}) fusion(bf16[4,5,64,192]{3,2,1,0:T(8,128)(2,1)S(1)} %get-tuple-element.67), kind=kLoop, calls=%fused_computation.48 | loop fusion | bytes 1179648 | tf_op jit(solution)/shard_map/slice | solution.py:33
  65.6 1.3 %collective-permute-start.8 = (bf16[4,6,1,192]{3,2,1,0:T(2,128)(2,1)S(1)}, bf16[4,6,1,192]{3,2,1,0:T(2,128)(2,1)S(1)}, u32[]{:S(2)}, u32[]{:S(2)}) collective-permute-start(bf16[4,6,1,192]{3,2,1,0:T(2,128)(2,1)S(1)} %get-tuple-element.50), channel_id=1, source_target_pairs={{0,1},{2,3},{4,5},{6,7},{8,9},{10,11},{12,13},{14,15},{16,17},{18,... | collective-permute-start | bytes 27656 | tf_op jit(solution)/shard_map/ppermute | solution.py:21
  66.9 1.3 %collective-permute-start.9 = (bf16[4,6,1,192]{3,2,1,0:T(2,128)(2,1)S(1)}, bf16[4,6,1,192]{3,2,1,0:T(2,128)(2,1)S(1)}, u32[]{:S(2)}, u32[]{:S(2)}) collective-permute-start(bf16[4,6,1,192]{3,2,1,0:T(2,128)(2,1)S(1)} %get-tuple-element.49), channel_id=1, source_target_pairs={{1,0},{3,2},{5,4},{7,6},{9,8},{11,10},{13,12},{15,14},{17,16},{19,... | collective-permute-start | bytes 27656 | tf_op jit(solution)/shard_map/ppermute | solution.py:23
  68.2 0.9 fusion.13
  69.1 0.0 collective-permute-done.8
  69.1 0.9 collective-permute-done.9
  70.0 0.4 pad_maximum_fusion.1
  70.4 1.7 %fusion.8 = (bf16[2,4,64,192]{3,2,1,0:T(8,128)(2,1)}, bf16[2,4,64,192]{3,2,1,0:T(8,128)(2,1)}, bf16[2,4,64,192]{3,2,1,0:T(8,128)(2,1)}, bf16[2,4,64,192]{3,2,1,0...) fusion(bf16[4,6,65,192]{3,2,1,0:T(8,128)(2,1)S(1)} %get-tuple-e, ...), kind=kLoop, calls=%fused_computation.44 | loop fusion | bytes 3538944 | tf_op jit(solution)/shard_map/slice | solution.py:33
  72.1 1.4 %fusion.9 = (bf16[2,4,64,192]{3,2,1,0:T(8,128)(2,1)}, bf16[2,4,64,192]{3,2,1,0:T(8,128)(2,1)}, bf16[2,4,64,192]{3,2,1,0:T(8,128)(2,1)}, bf16[2,4,64,192]{3,2,1,0...) fusion(bf16[4,6,65,192]{3,2,1,0:T(8,128)(2,1)S(1)} %get-tuple-e, ...), kind=kLoop, calls=%fused_computation.45 | loop fusion | bytes 3538944 | tf_op jit(solution)/shard_map/slice | solution.py:33
  73.5 2.8 %concatenate.112 = bf16[2,4,64,1728]{3,2,1,0:T(8,128)(2,1)S(1)} concatenate(bf16[2,4,64,192]{3,2,1,0:T(8,128)(2,1)} %get-tuple-element.26, bf16[2,4,64,192]{3,2,1,0:T(8,128)(2,1)} %get-tuple-element.60, bf16[2,4,64,192]{3,2,1,0:T(8,128)(2,1)} %get-tuple-element.17, bf16[2,4,64,192]{3,2,1,0:T(8,128)(2,1)} %get-tuple-element.25, bf16[2,4,64,192]{3,2,1,0:T(8,128)(2,1)S(1)} %pad_maximum_fusion.3, ...), dimensions={3} | concatenate | bytes 3538944 | tf_op jit(solution)/shard_map/concatenate | solution.py:37
  76.3 0.0 copy-start.1
  76.3 2.7 %fusion.17 = f32[512,192]{0,1:T(8,128)} fusion(bf16[512,1728]{1,0:T(8,128)(2,1)S(1)} %bitcast.29, bf16[1728,192]{1,0:T(8,128)(2,1)} %bitcast.35), kind=kOutput, calls=%fused_computation.53 | convolution fusion | flops 339738624 | bytes 2826240 | tf_op jit(solution)/shard_map/dot_general | solution.py:55
  79.0 0.0 copy-done.1
  79.0 2.7 %concatenate.113 = bf16[2,4,64,1728]{3,2,1,0:T(8,128)(2,1)S(1)} concatenate(bf16[2,4,64,192]{3,2,1,0:T(8,128)(2,1)} %get-tuple-element.23, bf16[2,4,64,192]{3,2,1,0:T(8,128)(2,1)} %get-tuple-element.59, bf16[2,4,64,192]{3,2,1,0:T(8,128)(2,1)} %get-tuple-element.14, bf16[2,4,64,192]{3,2,1,0:T(8,128)(2,1)} %get-tuple-element.22, ...), dimensions={3} | concatenate | bytes 3538944 | tf_op jit(solution)/shard_map/concatenate | solution.py:37
  81.8 2.7 %fusion.18 = f32[512,192]{0,1:T(8,128)} fusion(bf16[512,1728]{1,0:T(8,128)(2,1)S(1)} %bitcast.30, bf16[1728,192]{1,0:T(8,128)(2,1)} %bitcast.33), kind=kOutput, calls=%fused_computation.54 | convolution fusion | flops 339738624 | bytes 2826240 | tf_op jit(solution)/shard_map/dot_general | solution.py:55
  84.4 0.0 copy-start
  84.4 2.8 %concatenate.111 = bf16[2,4,64,1728]{3,2,1,0:T(8,128)(2,1)S(1)} concatenate(bf16[2,4,64,192]{3,2,1,0:T(8,128)(2,1)} %get-tuple-element.28, bf16[2,4,64,192]{3,2,1,0:T(8,128)(2,1)} %get-tuple-element.58, bf16[2,4,64,192]{3,2,1,0:T(8,128)(2,1)} %get-tuple-element.19, bf16[2,4,64,192]{3,2,1,0:T(8,128)(2,1)} %get-tuple-element.27, ...), dimensions={3} | concatenate | bytes 3538944 | tf_op jit(solution)/shard_map/concatenate | solution.py:37
  87.3 0.0 copy-done
  87.3 0.0 copy-start.4
  87.3 2.5 %multiply_reduce_fusion = (f32[512]{0:T(512)S(1)}, f32[512,192]{0,1:T(8,128)}) fusion(f32[512,192]{0,1:T(8,128)} %fusion.18, f32[512,192]{0,1:T(8,128)S(1)} %copy-done, bf16[512,1728]{1,0:T(8,128)(2,1)S(1)} %bitcast.27, bf16[1728,192]{1,0:T(8,128)(2,1)S(1)} %bitcast.32), kind=kOutput, calls=%fused_computation.20 | convolution fusion | flops 340131328 | bytes 3614720 | tf_op jit(solution)/shard_map/dot_general | solution.py:55
  89.8 1.2 %copy.9 = f32[512,192]{1,0:T(8,128)S(1)} copy(f32[512,192]{0,1:T(8,128)} %get-tuple-element.80) | data formatting | bytes 786432 | tf_op jit(solution)/shard_map/add | solution.py:55
  91.0 0.1 rsqrt.25
  91.1 0.0 copy-done.4
  91.1 0.9 multiply_convert_fusion
  (8 shorter events, 0.2 us)
Async XLA Ops:
  0.0 10.8 %collective-permute-start = (bf16[2,4,64,192]{3,2,1,0:T(8,128)(2,1)}, bf16[2,4,64,192]{3,2,1,0:T(8,128)(2,1)S(1)}, u32[]{:S(2)}, u32[]{:S(2)}) collective-permute-start(bf16[2,4,64,192]{3,2,1,0:T(8,128)(2,1)} %param.5), channel_id=1, source_target_pairs={{0,4},{4,8},{8,12},{1,5},{5,9},{9,13},{2,6},{6,10},{10,14},{3,7},{... | collective-permute-start | bytes 589832 | tf_op jit(solution)/shard_map/ppermute | solution.py:10
  10.8 4.5 %copy-start.2 = (bf16[2,4,64,192]{3,2,1,0:T(8,128)(2,1)}, bf16[2,4,64,192]{3,2,1,0:T(8,128)(2,1)S(1)}, u32[]{:S(2)}) copy-start(bf16[2,4,64,192]{3,2,1,0:T(8,128)(2,1)S(1)} %collective-permute-done) | copy-start | bytes 589828
  11.9 7.9 %collective-permute-start.1 = (bf16[4,1,64,192]{3,2,1,0:T(8,128)(2,1)S(1)}, bf16[4,1,64,192]{3,2,1,0:T(8,128)(2,1)S(1)}, u32[]{:S(2)}, u32[]{:S(2)}) collective-permute-start(bf16[4,1,64,192]{3,2,1,0:T(8,128)(2,1)S(1)} %get-tuple-element.75), channel_id=1, source_target_pairs={{0,2},{1,3},{4,6},{5,7},{8,10},{9,11},{12,14},{13,15},{16,18},{17,... | collective-permute-start | bytes 294920 | tf_op jit(solution)/shard_map/ppermute | solution.py:21
  15.4 6.9 %collective-permute-start.2 = (bf16[4,1,64,192]{3,2,1,0:T(8,128)(2,1)S(1)}, bf16[4,1,64,192]{3,2,1,0:T(8,128)(2,1)S(1)}, u32[]{:S(2)}, u32[]{:S(2)}) collective-permute-start(bf16[4,1,64,192]{3,2,1,0:T(8,128)(2,1)S(1)} %get-tuple-element.76), channel_id=1, source_target_pairs={{2,0},{3,1},{6,4},{7,5},{10,8},{11,9},{14,12},{15,13},{18,16},{19,... | collective-permute-start | bytes 294920 | tf_op jit(solution)/shard_map/ppermute | solution.py:23
  22.3 3.9 %collective-permute-start.3 = (bf16[4,6,1,192]{3,2,1,0:T(2,128)(2,1)S(1)}, bf16[4,6,1,192]{3,2,1,0:T(2,128)(2,1)S(1)}, u32[]{:S(2)}, u32[]{:S(2)}) collective-permute-start(bf16[4,6,1,192]{3,2,1,0:T(2,128)(2,1)S(1)} %get-tuple-element.54), channel_id=1, source_target_pairs={{0,1},{2,3},{4,5},{6,7},{8,9},{10,11},{12,13},{14,15},{16,17},{18,... | collective-permute-start | bytes 27656 | tf_op jit(solution)/shard_map/ppermute | solution.py:21
  23.6 3.1 %collective-permute-start.4 = (bf16[4,6,1,192]{3,2,1,0:T(2,128)(2,1)S(1)}, bf16[4,6,1,192]{3,2,1,0:T(2,128)(2,1)S(1)}, u32[]{:S(2)}, u32[]{:S(2)}) collective-permute-start(bf16[4,6,1,192]{3,2,1,0:T(2,128)(2,1)S(1)} %get-tuple-element.53), channel_id=1, source_target_pairs={{1,0},{3,2},{5,4},{7,6},{9,8},{11,10},{13,12},{15,14},{17,16},{19,... | collective-permute-start | bytes 27656 | tf_op jit(solution)/shard_map/ppermute | solution.py:23
  41.5 2.8 %copy-start.3 = (f32[192]{0:T(256)S(1)}, f32[192]{0:T(256)}, u32[]{:S(2)}) copy-start(f32[192]{0:T(256)} %param.7) | copy-start | bytes 2308
  44.6 10.7 %collective-permute-start.5 = (bf16[2,4,64,192]{3,2,1,0:T(8,128)(2,1)S(1)}, bf16[2,4,64,192]{3,2,1,0:T(8,128)(2,1)S(1)}, u32[]{:S(2)}, u32[]{:S(2)}) collective-permute-start(bf16[2,4,64,192]{3,2,1,0:T(8,128)(2,1)S(1)} %multiply_convert_fusion.1), channel_id=1, source_target_pairs={{0,4},{4,8},{8,12},{1,5},{5,9},{9,13},{2,6},{6,10},{10,14},{3,7},{... | collective-permute-start | bytes 589832 | tf_op jit(solution)/shard_map/ppermute | solution.py:10
  55.3 4.9 %collective-permute-start.6 = (bf16[4,1,64,192]{3,2,1,0:T(8,128)(2,1)S(1)}, bf16[4,1,64,192]{3,2,1,0:T(8,128)(2,1)S(1)}, u32[]{:S(2)}, u32[]{:S(2)}) collective-permute-start(bf16[4,1,64,192]{3,2,1,0:T(8,128)(2,1)S(1)} %get-tuple-element.69), channel_id=1, source_target_pairs={{0,2},{1,3},{4,6},{5,7},{8,10},{9,11},{12,14},{13,15},{16,18},{17,... | collective-permute-start | bytes 294920 | tf_op jit(solution)/shard_map/ppermute | solution.py:21
  57.5 6.9 %collective-permute-start.7 = (bf16[4,1,64,192]{3,2,1,0:T(8,128)(2,1)S(1)}, bf16[4,1,64,192]{3,2,1,0:T(8,128)(2,1)S(1)}, u32[]{:S(2)}, u32[]{:S(2)}) collective-permute-start(bf16[4,1,64,192]{3,2,1,0:T(8,128)(2,1)S(1)} %get-tuple-element.70), channel_id=1, source_target_pairs={{2,0},{3,1},{6,4},{7,5},{10,8},{11,9},{14,12},{15,13},{18,16},{19,... | collective-permute-start | bytes 294920 | tf_op jit(solution)/shard_map/ppermute | solution.py:23
  65.6 3.5 %collective-permute-start.8 = (bf16[4,6,1,192]{3,2,1,0:T(2,128)(2,1)S(1)}, bf16[4,6,1,192]{3,2,1,0:T(2,128)(2,1)S(1)}, u32[]{:S(2)}, u32[]{:S(2)}) collective-permute-start(bf16[4,6,1,192]{3,2,1,0:T(2,128)(2,1)S(1)} %get-tuple-element.50), channel_id=1, source_target_pairs={{0,1},{2,3},{4,5},{6,7},{8,9},{10,11},{12,13},{14,15},{16,17},{18,... | collective-permute-start | bytes 27656 | tf_op jit(solution)/shard_map/ppermute | solution.py:21
  66.9 3.1 %collective-permute-start.9 = (bf16[4,6,1,192]{3,2,1,0:T(2,128)(2,1)S(1)}, bf16[4,6,1,192]{3,2,1,0:T(2,128)(2,1)S(1)}, u32[]{:S(2)}, u32[]{:S(2)}) collective-permute-start(bf16[4,6,1,192]{3,2,1,0:T(2,128)(2,1)S(1)} %get-tuple-element.49), channel_id=1, source_target_pairs={{1,0},{3,2},{5,4},{7,6},{9,8},{11,10},{13,12},{15,14},{17,16},{19,... | collective-permute-start | bytes 27656 | tf_op jit(solution)/shard_map/ppermute | solution.py:23
  76.3 2.7 %copy-start.1 = (bf16[2,4,64,192]{3,2,1,0:T(8,128)(2,1)S(1)}, bf16[2,4,64,192]{3,2,1,0:T(8,128)(2,1)}, u32[]{:S(2)}) copy-start(bf16[2,4,64,192]{3,2,1,0:T(8,128)(2,1)} %get-tuple-element.12) | copy-start | bytes 589828
  84.4 2.8 %copy-start = (f32[512,192]{0,1:T(8,128)S(1)}, f32[512,192]{0,1:T(8,128)}, u32[]{:S(2)}) copy-start(f32[512,192]{0,1:T(8,128)} %fusion.17) | copy-start | bytes 1179652
  87.3 3.8 %copy-start.4 = (f32[192]{0:T(256)S(1)}, f32[192]{0:T(256)}, u32[]{:S(2)}) copy-start(f32[192]{0:T(256)} %param.9) | copy-start | bytes 2308
where the time goes:
time: 93.4 us; the launch traced here: 92 us
  local copies, waits for them, and re-layouts  33.8 us (36%)
  starting transfers between devices  22.6 us (24%)
  waiting for transfers between devices  18.3 us (20%)
  matrix products  13.3 us (14%)
  other arithmetic  3.8 us (4%)
    concatenate x6, local copies, waits for them, and re-layouts, tap_block(): return jnp.concatenate(pieces, axis=-1).reshape(count * rows * cols, -1)  16.8 us
    dot_general x6, matrix products, conv_layer(): jnp.dot(tap_block(padded[offset_t:offset_t + frames], rows, cols), flat_w...  13.3 us
    ppermute x2, starting transfers between devices, from_behind(): return lax.ppermute(x, axis, pairs)  9.26 us
    ppermute x2, waiting for transfers between devices, from_behind(): return lax.ppermute(x, axis, pairs)  9.05 us
    ppermute x4, starting transfers between devices, with_halo(): lax.ppermute(tail, axis, [(i, (i + 1) % count) for i in range(ends)])  8.17 us
    ppermute x4, waiting for transfers between devices, with_halo(): lax.ppermute(head, axis, [((i + 1) % count, i) for i in range(ends)])  7.86 us
    slice x5, local copies, waits for them, and re-layouts, tap_block(): block[:, offset_y:offset_y + rows, offset_x:offset_x + cols]  7 us
    slice x2, local copies, waits for them, and re-layouts, conv_layer(): flat_weight[offset_t]  6.35 us
  transfers between devices with their start and end apart: 10, of which 7 were waited for; matrix products, arithmetic and copies ran while one was open for 9% of the time, Pallas kernels for 0%

commit v1 on v0

v1 whole, which is shorter than its diff:
```python
import functools

import jax
import jax.numpy as jnp
from jax import lax
from jax.experimental import pallas as pl
from jax.experimental.pallas import tpu as pltpu
from jax.sharding import PartitionSpec as P

MESH = pl.DeviceIdType.MESH
AXES = ("frame", "strip", "slab")


def exists(position, sizes, offsets):
    checks = []
    for index, size, offset in zip(position, sizes, offsets):
        if abs(offset) >= size:
            return None
        if offset > 0:
            checks.append(index < size - offset)
        elif offset < 0:
            checks.append(index >= -offset)
    return functools.reduce(jnp.logical_and, checks) if checks else True


def guarded(condition, action):
    if condition is None:
        return
    if condition is True:
        action()
    else:
        pl.when(condition)(action)


def kernel(
    sizes,
    x_ref,
    w1_hbm,
    s1_ref,
    w2_hbm,
    s2_ref,
    out_ref,
    weights,
    hidden,
    edges,
    mains,
    rows,
    tiles,
    taps,
    weight_sem,
    send_sem,
    recv_sem,
):
    frames, height, width, channels = x_ref.shape
    cells = height * width
    position = tuple(lax.axis_index(axis) for axis in AXES)

    def at(offsets):
        return {axis: index + offset for axis, index, offset in zip(AXES, position, offsets)}

    around = [(dz, ds, db) for dz in (0, 1) for ds in (-1, 0, 1) for db in (-1, 0, 1) if (dz, ds, db) != (0, 0, 0)]

    loads = []
    for layer, source in enumerate((w1_hbm, w2_hbm)):
        for offset_t in (2, 1, 0):
            copy = pltpu.make_async_copy(source.at[offset_t], weights.at[layer, offset_t], weight_sem.at[layer, offset_t])
            copy.start()
            loads.append(copy)
    loads = {(i // 3, 2 - i % 3): copy for i, copy in enumerate(loads)}

    def zero(ref, condition):
        def clear():
            ref[...] = jnp.zeros_like(ref)

        if condition is None:
            clear()
        elif condition is not True:
            pl.when(jnp.logical_not(condition))(clear)

    for layer in range(2):
        for slot in range(2 * frames):
            dz = 1 if slot < frames else 0
            if dz:
                zero(mains.at[layer, slot], exists(position, sizes, (-1, 0, 0)))
            for k, ds in ((0, 1), (1, -1)):
                zero(rows.at[layer, slot, k], exists(position, sizes, (-dz, -ds, 0)))
            for k in range(3):
                for side, db in ((0, 1), (1, -1)):
                    zero(tiles.at[layer, slot, k, side], exists(position, sizes, (-dz, k - 1, -db)))

    barrier = pltpu.get_barrier_semaphore()
    for offsets in around:
        back = tuple(-o for o in offsets)
        guarded(
            exists(position, sizes, back),
            lambda back=back: pl.semaphore_signal(barrier, inc=1, device_id=at(back), device_id_type=MESH),
        )

    def piece(layer, frame, main, offsets):
        dz, ds, db = offsets
        slot = frame if dz else frames + frame
        if db == 0 and ds == 0:
            src, dst, kind = main, mains.at[layer, slot], 0
        elif db == 0:
            row = height - 1 if ds > 0 else 0
            k = 0 if ds > 0 else 1
            src, dst, kind = main.at[row], rows.at[layer, slot, k], 1 + k
        else:
            side = 0 if db > 0 else 1
            src = edges.at[layer, frame, side]
            dst, kind = tiles.at[layer, slot, 1 - ds, side], 3 + 2 * (1 - ds) + side
        return pltpu.make_async_remote_copy(
            src_ref=src,
            dst_ref=dst,
            send_sem=send_sem.at[layer, slot, kind],
            recv_sem=recv_sem.at[layer, slot, kind],
            device_id=at(offsets),
            device_id_type=MESH,
        )

    def fill_edges(layer, frame, block):
        for side, column in ((0, width - 1), (1, 0)):
            picked = jnp.concatenate([block[r, column : column + 1] for r in range(height)], axis=0)
            edges[layer, frame, side, 0:height] = picked.astype(jnp.bfloat16)

    def send(layer, frame, main):
        order = sorted(around, key=lambda o: (-o[0], o[2] == 0, o[1] == 0))
        for offsets in order:
            guarded(exists(position, sizes, offsets), lambda o=offsets: piece(layer, frame, main, o).start())

    def receive(layer, slot, main):
        dz = 1 if slot < frames else 0
        for offsets in around:
            if offsets[0] != dz:
                continue
            back = tuple(-o for o in offsets)
            guarded(exists(position, sizes, back), lambda o=offsets: piece(layer, slot % frames, main, o).wait_recv())

    def gather(layer, slot, block_ref):
        top = rows[layer, slot, 0][None].astype(jnp.float32)
        bottom = rows[layer, slot, 1][None].astype(jnp.float32)
        block = jnp.concatenate([top, block_ref[...].astype(jnp.float32), bottom], axis=0)
        halo = []
        for side in range(2):
            above = tiles[layer, slot, 0, side].astype(jnp.float32)
            level = tiles[layer, slot, 1, side].astype(jnp.float32)
            below = tiles[layer, slot, 2, side].astype(jnp.float32)
            picked = [above[height - 1 : height]] + [level[r : r + 1] for r in range(height)] + [below[0:1]]
            halo.append(jnp.stack(picked, axis=0))
        column = lax.broadcasted_iota(jnp.int32, block.shape, 1)
        before = jnp.where(column == 0, halo[0], pltpu.roll(block, 1, 1))
        after = jnp.where(column == width - 1, halo[1], pltpu.roll(block, width - 1, 1))
        shifted = [part.astype(jnp.bfloat16) for part in (before, block, after)]
        pieces = [shifted[x][y : y + height].reshape(cells, channels) for y in range(3) for x in range(3)]
        taps[slot] = jnp.concatenate(pieces, axis=-1)

    def product(layer, slot, offset_t):
        return jnp.dot(taps[slot], weights[layer, offset_t], preferred_element_type=jnp.float32)

    def finish(convolved, scale_ref):
        mean_square = jnp.sum(convolved * convolved, axis=-1, keepdims=True) * (1.0 / channels)
        normed = convolved * lax.rsqrt(mean_square + 1e-06) * scale_ref[...]
        return (normed / (1.0 + jnp.exp(-normed))).reshape(height, width, channels)

    for frame in (1, 0):
        fill_edges(0, frame, x_ref.at[frame][...].astype(jnp.float32))

    count = jnp.int32(0)
    for offsets in around:
        condition = exists(position, sizes, offsets)
        if condition is not None:
            count = count + (1 if condition is True else condition.astype(jnp.int32))
    pl.semaphore_wait(barrier, count)

    for frame in (1, 0):
        send(0, frame, x_ref.at[frame])

    def conv_layer(layer, source, scale_ref, emit):
        for slot in (3, 2):
            receive(layer, slot, source.at[slot - 2])
            gather(layer, slot, source.at[slot - 2])
        loads[layer, 2].wait()
        late = product(layer, 3, 2)
        early = product(layer, 2, 2)
        loads[layer, 1].wait()
        late = late + product(layer, 2, 1)
        receive(layer, 1, source.at[1])
        gather(layer, 1, mains.at[layer, 1])
        loads[layer, 0].wait()
        emit(1, finish(late + product(layer, 1, 0), scale_ref))
        early = early + product(layer, 1, 1)
        receive(layer, 0, source.at[0])
        gather(layer, 0, mains.at[layer, 0])
        emit(0, finish(early + product(layer, 0, 0), scale_ref))

    def emit_hidden(frame, values):
        hidden[frame] = values.astype(jnp.bfloat16)
        fill_edges(1, frame, values)
        send(1, frame, hidden.at[frame])

    def emit_output(frame, values):
        out_ref[frame] = values.astype(jnp.bfloat16)

    conv_layer(0, x_ref, s1_ref, emit_hidden)
    conv_layer(1, hidden, s2_ref, emit_output)

    for layer, source in ((0, x_ref), (1, hidden)):
        for frame in (1, 0):
            for offsets in around:
                guarded(
                    exists(position, sizes, offsets),
                    lambda o=offsets: piece(layer, frame, source.at[frame], o).wait_send(),
                )


def shards(sizes, frames_in, weight_first, scale_first, weight_second, scale_second):
    frames, height, width, channels = frames_in.shape
    vmem, anywhere = pl.BlockSpec(memory_space=pltpu.VMEM), pl.BlockSpec(memory_space=pl.ANY)
    flat = (3, 9 * channels, channels)
    half = jnp.bfloat16
    return pl.pallas_call(
        functools.partial(kernel, sizes),
        out_shape=jax.ShapeDtypeStruct(frames_in.shape, half),
        in_specs=[vmem, anywhere, vmem, anywhere, vmem],
        out_specs=vmem,
        scratch_shapes=[
            pltpu.VMEM((2, *flat), half),
            pltpu.VMEM(frames_in.shape, half),
            pltpu.VMEM((2, frames, 2, 8, channels), half),
            pltpu.VMEM((2, frames, height, width, channels), half),
            pltpu.VMEM((2, 2 * frames, 2, width, channels), half),
            pltpu.VMEM((2, 2 * frames, 3, 2, 8, channels), half),
            pltpu.VMEM((2 * frames, height * width, 9 * channels), half),
            pltpu.SemaphoreType.DMA((2, 3)),
            pltpu.SemaphoreType.DMA((2, 2 * frames, 9)),
            pltpu.SemaphoreType.DMA((2, 2 * frames, 9)),
        ],
        compiler_params=pltpu.CompilerParams(collective_id=0, has_side_effects=True),
        name="conv_block",
    )(
        frames_in,
        weight_first.reshape(flat),
        scale_first.reshape(1, channels),
        weight_second.reshape(flat),
        scale_second.reshape(1, channels),
    )


def solution(mesh):
    sizes = tuple(mesh.shape[axis] for axis in AXES)
    return jax.shard_map(
        functools.partial(shards, sizes),
        mesh=mesh,
        in_specs=(P(("groups", "frame"), "strip", "slab", None), P(), P(), P(), P()),
        out_specs=P(("groups", "frame"), "strip", "slab", None),
        check_vma=False,
    )
```

time: 93.4 us -> 24.7 us (0.26)
  local copies, waits for them, and re-layouts: 33.8 us -> 1.67 us
  Pallas kernels: 0 us -> 22.6 us
  starting transfers between devices: 22.6 us -> 0 us
  waiting for transfers between devices: 18.3 us -> 0 us
  matrix products: 13.3 us -> 0 us
  other arithmetic: 3.8 us -> 0 us
    ppermute x10 -> x0, starting transfers between devices: 22.6 us -> none  [the longest x2 9.26 us: from_behind(): return lax.ppermute(x, axis, pairs)]
    pallas_call x0 -> x1, Pallas kernels: none -> 22.6 us  [shards(): pl.pallas_call(functools.partial(kernel, sizes), out_shape=jax.ShapeDtype...]
    ppermute x10 -> x0, waiting for transfers between devices: 18.3 us -> none  [the longest x2 9.05 us: from_behind(): return lax.ppermute(x, axis, pairs)]
    concatenate x7 -> x0, local copies, waits for them, and re-layouts: 17.9 us -> none  [the longest x6 16.8 us: tap_block(): return jnp.concatenate(pieces, axis=-1).reshape(count * rows * cols, -1)]
    slice x8 -> x0, local copies, waits for them, and re-layouts: 13.4 us -> none  [the longest x5 7 us: tap_block(): block[:, offset_y:offset_y + rows, offset_x:offset_x + cols]]
    dot_general x6 -> x0, matrix products: 13.3 us -> none  [conv_layer(): jnp.dot(tap_block(padded[offset_t:offset_t + frames], rows, cols), flat_w...]
    concatenate x7 -> x0, other arithmetic: 2.6 us -> none  [the longest x6 2.56 us: with_halo(): jnp.concatenate([lax.ppermute(tail, axis, [(i, (i + 1) % count) for i in...]
    add x2 -> x0, local copies, waits for them, and re-layouts: 2.38 us -> none  [conv_layer(): accumulated + jnp.dot(tap_block(padded[offset_t:offset_t + frames], rows,...]
  transfers between devices with their start and end apart: 10 -> 0, of which waited for: 7 -> 0; matrix products, arithmetic and copies ran while one was open for 9% -> 0% of each run, Pallas kernels for 0% -> 0%
where the time goes in v1:
time: 24.7 us; the launch traced here: 24.3 us
  Pallas kernels  22.6 us (91%)
  local copies, waits for them, and re-layouts  1.67 us (7%)
    pallas_call x1, Pallas kernels, shards(): pl.pallas_call(functools.partial(kernel, sizes), out_shape=jax.ShapeDtype...  22.6 us
    unnamed x1, local copies, waits for them, and re-layouts  1.67 us

profile of v1, /device:TPU:0, one launch (start us, length us, event | category | flops | bytes accessed | tf_op | source)
XLA Modules:
  0.0 24.3 jit_solution(5391288473337102493)
XLA Ops:
  0.0 22.6 %conv_block.1 = bf16[2,4,64,192]{3,2,1,0:T(8,128)(2,1)} custom-call(bf16[2,4,64,192]{3,2,1,0:T(8,128)(2,1)} %x_ref.1, bf16[3,1728,192]{2,1,0:T(8,128)(2,1)} %bitcast.4, f32[1,192]{1,0:T(1,128)} %bitcast.6, bf16[3,1728,192]{2,1,0:T(8,128)(2,1)} %bitcast.5, f32[1,192]{1,0:T(1,128)} %bitcast.7), custom_call_target="tpu_custom_call" | custom-call | tf_op jit(solution)/shard_map/conv_block/pallas_call | solution.py:221
  22.6 1.7 %copy.7 = bf16[2,4,64,192]{3,2,1,0:T(8,128)(2,1)} copy(bf16[2,4,64,192]{3,2,1,0:T(8,128)(2,1)} %conv_block.1) | data formatting | bytes 393216

commit v2 on v1

--- a/solution.py
+++ b/solution.py
@@ -32,21 +32,37 @@
         pl.when(condition)(action)
 
 
+def pack(block):
+    lead, half = 128, block.shape[1] // 2
+    rest = block[..., lead:]
+    return jnp.concatenate([block[..., :lead], jnp.concatenate([rest[:, :half], rest[:, half:]], axis=-1)], axis=1)
+
+
+def unpack(packed, width):
+    rest, lanes = packed[:, width:], packed.shape[-1] // 2
+    rest = jnp.concatenate([rest[..., :lanes], rest[..., lanes:]], axis=1)
+    return jnp.concatenate([packed[:, :width], rest], axis=-1)
+
+
 def kernel(
     sizes,
+    x_hbm,
+    w1_hbm,
+    s1_hbm,
+    w2_hbm,
+    s2_hbm,
+    out_ref,
     x_ref,
-    w1_hbm,
-    s1_ref,
-    w2_hbm,
-    s2_ref,
-    out_ref,
+    scales,
+    staged,
     weights,
-    hidden,
+    packs,
     edges,
     mains,
     rows,
     tiles,
     taps,
+    local_sem,
     weight_sem,
     send_sem,
     recv_sem,
@@ -60,6 +76,18 @@
 
     around = [(dz, ds, db) for dz in (0, 1) for ds in (-1, 0, 1) for db in (-1, 0, 1) if (dz, ds, db) != (0, 0, 0)]
 
+    barrier = pltpu.get_barrier_semaphore()
+    for offsets in around:
+        back = tuple(-o for o in offsets)
+        guarded(
+            exists(position, sizes, back),
+            lambda back=back: pl.semaphore_signal(barrier, inc=1, device_id=at(back), device_id_type=MESH),
+        )
+
+    x_loads = [pltpu.make_async_copy(x_hbm.at[frame], x_ref.at[frame], local_sem.at[frame]) for frame in range(2)]
+    for frame in (1, 0):
+        x_loads[frame].start()
+
     loads = []
     for layer, source in enumerate((w1_hbm, w2_hbm)):
         for offset_t in (2, 1, 0):
@@ -67,34 +95,10 @@
             copy.start()
             loads.append(copy)
     loads = {(i // 3, 2 - i % 3): copy for i, copy in enumerate(loads)}
-
-    def zero(ref, condition):
-        def clear():
-            ref[...] = jnp.zeros_like(ref)
-
-        if condition is None:
-            clear()
-        elif condition is not True:
-            pl.when(jnp.logical_not(condition))(clear)
-
-    for layer in range(2):
-        for slot in range(2 * frames):
-            dz = 1 if slot < frames else 0
-            if dz:
-                zero(mains.at[layer, slot], exists(position, sizes, (-1, 0, 0)))
-            for k, ds in ((0, 1), (1, -1)):
-                zero(rows.at[layer, slot, k], exists(position, sizes, (-dz, -ds, 0)))
-            for k in range(3):
-                for side, db in ((0, 1), (1, -1)):
-                    zero(tiles.at[layer, slot, k, side], exists(position, sizes, (-dz, k - 1, -db)))
-
-    barrier = pltpu.get_barrier_semaphore()
-    for offsets in around:
-        back = tuple(-o for o in offsets)
-        guarded(
-            exists(position, sizes, back),
-            lambda back=back: pl.semaphore_signal(barrier, inc=1, device_id=at(back), device_id_type=MESH),
-        )
+    scale_loads = [pltpu.make_async_copy(ref, scales.at[layer], local_sem.at[2 + layer]) for layer, ref in enumerate((s1_hbm, s2_hbm))]
+    for copy in scale_loads:
+        copy.start()
+    out_copies = [pltpu.make_async_copy(staged.at[frame], out_ref.at[frame], local_sem.at[4 + frame]) for frame in range(2)]
 
     def piece(layer, frame, main, offsets):
         dz, ds, db = offsets
@@ -124,7 +128,7 @@
             edges[layer, frame, side, 0:height] = picked.astype(jnp.bfloat16)
 
     def send(layer, frame, main):
-        order = sorted(around, key=lambda o: (-o[0], o[2] == 0, o[1] == 0))
+        order = sorted(around, key=lambda o: (o[0], o[2] == 0, o[1] == 0))
         for offsets in order:
             guarded(exists(position, sizes, offsets), lambda o=offsets: piece(layer, frame, main, o).start())
 
@@ -137,9 +141,8 @@
             guarded(exists(position, sizes, back), lambda o=offsets: piece(layer, slot % frames, main, o).wait_recv())
 
     def gather(layer, slot, block_ref):
-        top = rows[layer, slot, 0][None].astype(jnp.float32)
-        bottom = rows[layer, slot, 1][None].astype(jnp.float32)
-        block = jnp.concatenate([top, block_ref[...].astype(jnp.float32), bottom], axis=0)
+        block = jnp.concatenate([rows[layer, slot, 0][None], block_ref[...], rows[layer, slot, 1][None]], axis=0)
+        block = unpack(block, width).astype(jnp.float32)
         halo = []
         for side in range(2):
             above = tiles[layer, slot, 0, side].astype(jnp.float32)
@@ -157,13 +160,15 @@
     def product(layer, slot, offset_t):
         return jnp.dot(taps[slot], weights[layer, offset_t], preferred_element_type=jnp.float32)
 
-    def finish(convolved, scale_ref):
+    def finish(convolved, layer):
         mean_square = jnp.sum(convolved * convolved, axis=-1, keepdims=True) * (1.0 / channels)
-        normed = convolved * lax.rsqrt(mean_square + 1e-06) * scale_ref[...]
+        normed = convolved * lax.rsqrt(mean_square + 1e-06) * scales[layer]
         return (normed / (1.0 + jnp.exp(-normed))).reshape(height, width, channels)
 
     for frame in (1, 0):
-        fill_edges(0, frame, x_ref.at[frame][...].astype(jnp.float32))
+        x_loads[frame].wait()
+        packs[0, frame] = pack(x_ref[frame])
+        fill_edges(0, frame, x_ref[frame].astype(jnp.float32))
 
     count = jnp.int32(0)
     for offsets in around:
@@ -173,9 +178,31 @@
     pl.semaphore_wait(barrier, count)
 
     for frame in (1, 0):
-        send(0, frame, x_ref.at[frame])
-
-    def conv_layer(layer, source, scale_ref, emit):
+        send(0, frame, packs.at[0, frame])
+
+    def zero(ref, condition):
+        def clear():
+            ref[...] = jnp.zeros_like(ref)
+
+        if condition is None:
+            clear()
+        elif condition is not True:
+            pl.when(jnp.logical_not(condition))(clear)
+
+    for layer in range(2):
+        for slot in range(2 * frames):
+            dz = 1 if slot < frames else 0
+            if dz:
+                zero(mains.at[layer, slot], exists(position, sizes, (-1, 0, 0)))
+            for k, ds in ((0, 1), (1, -1)):
+                zero(rows.at[layer, slot, k], exists(position, sizes, (-dz, -ds, 0)))
+            for k in range(3):
+                for side, db in ((0, 1), (1, -1)):
+                    zero(tiles.at[layer, slot, k, side], exists(position, sizes, (-dz, k - 1, -db)))
+    for copy in scale_loads:
+        copy.wait()
+
+    def conv_layer(layer, source, emit):
         for slot in (3, 2):
             receive(layer, slot, source.at[slot - 2])
             gather(layer, slot, source.at[slot - 2])
@@ -187,50 +214,58 @@
         receive(layer, 1, source.at[1])
         gather(layer, 1, mains.at[layer, 1])
         loads[layer, 0].wait()
-        emit(1, finish(late + product(layer, 1, 0), scale_ref))
+        emit(1, finish(late + product(layer, 1, 0), layer))
         early = early + product(layer, 1, 1)
         receive(layer, 0, source.at[0])
         gather(layer, 0, mains.at[layer, 0])
-        emit(0, finish(early + product(layer, 0, 0), scale_ref))
+        emit(0, finish(early + product(layer, 0, 0), layer))
 
     def emit_hidden(frame, values):
-        hidden[frame] = values.astype(jnp.bfloat16)
+        packs[1, frame] = pack(values).astype(jnp.bfloat16)
         fill_edges(1, frame, values)
-        send(1, frame, hidden.at[frame])
+        send(1, frame, packs.at[1, frame])
 
     def emit_output(frame, values):
-        out_ref[frame] = values.astype(jnp.bfloat16)
-
-    conv_layer(0, x_ref, s1_ref, emit_hidden)
-    conv_layer(1, hidden, s2_ref, emit_output)
-
-    for layer, source in ((0, x_ref), (1, hidden)):
+        staged[frame] = values.astype(jnp.bfloat16)
+        out_copies[frame].start()
+
+    conv_layer(0, packs.at[0], emit_hidden)
+    conv_layer(1, packs.at[1], emit_output)
+
+    for layer in range(2):
         for frame in (1, 0):
             for offsets in around:
                 guarded(
                     exists(position, sizes, offsets),
-                    lambda o=offsets: piece(layer, frame, source.at[frame], o).wait_send(),
+                    lambda o=offsets: piece(layer, frame, packs.at[layer, frame], o).wait_send(),
                 )
+    for copy in out_copies:
+        copy.wait()
 
 
 def shards(sizes, frames_in, weight_first, scale_first, weight_second, scale_second):
     frames, height, width, channels = frames_in.shape
-    vmem, anywhere = pl.BlockSpec(memory_space=pltpu.VMEM), pl.BlockSpec(memory_space=pl.ANY)
+    anywhere = pl.BlockSpec(memory_space=pl.ANY)
+    lines = width * channels // 128
     flat = (3, 9 * channels, channels)
     half = jnp.bfloat16
     return pl.pallas_call(
         functools.partial(kernel, sizes),
         out_shape=jax.ShapeDtypeStruct(frames_in.shape, half),
-        in_specs=[vmem, anywhere, vmem, anywhere, vmem],
-        out_specs=vmem,
+        in_specs=[anywhere] * 5,
+        out_specs=anywhere,
         scratch_shapes=[
+            pltpu.VMEM(frames_in.shape, half),
+            pltpu.VMEM((2, 1, channels), jnp.float32),
+            pltpu.VMEM(frames_in.shape, half),
             pltpu.VMEM((2, *flat), half),
-            pltpu.VMEM(frames_in.shape, half),
+            pltpu.VMEM((2, frames, height, lines, 128), half),
             pltpu.VMEM((2, frames, 2, 8, channels), half),
-            pltpu.VMEM((2, frames, height, width, channels), half),
-            pltpu.VMEM((2, 2 * frames, 2, width, channels), half),
+            pltpu.VMEM((2, frames, height, lines, 128), half),
+            pltpu.VMEM((2, 2 * frames, 2, lines, 128), half),
             pltpu.VMEM((2, 2 * frames, 3, 2, 8, channels), half),
             pltpu.VMEM((2 * frames, height * width, 9 * channels), half),
+            pltpu.SemaphoreType.DMA((6,)),
             pltpu.SemaphoreType.DMA((2, 3)),
             pltpu.SemaphoreType.DMA((2, 2 * frames, 9)),
             pltpu.SemaphoreType.DMA((2, 2 * frames, 9)),

time: 24.7 us -> 21.7 us (0.88); the launches traced: 24.3 us -> 21.5 us
  Pallas kernels: 22.6 us -> 19.9 us
    pallas_call x1, Pallas kernels: 22.6 us -> 19.9 us  [shards(): pl.pallas_call(functools.partial(kernel, sizes), out_shape=jax.ShapeDtype...]
where the time goes in v2:
time: 21.7 us; the launch traced here: 21.5 us
  Pallas kernels  19.9 us (92%)
  local copies, waits for them, and re-layouts  1.67 us (8%)
    pallas_call x1, Pallas kernels, shards(): pl.pallas_call(functools.partial(kernel, sizes), out_shape=jax.ShapeDtype...  19.9 us
    unnamed x1, local copies, waits for them, and re-layouts  1.67 us

profile of v2, /device:TPU:0, one launch (start us, length us, event | category | flops | bytes accessed | tf_op | source)
XLA Modules:
  0.0 21.5 jit_solution(8553395202179051283)
XLA Ops:
  0.0 19.9 %conv_block.1 = bf16[2,4,64,192]{3,2,1,0:T(8,128)(2,1)} custom-call(bf16[2,4,64,192]{3,2,1,0:T(8,128)(2,1)} %x_hbm.1, bf16[3,1728,192]{2,1,0:T(8,128)(2,1)} %bitcast.4, f32[1,192]{1,0:T(1,128)} %bitcast.6, bf16[3,1728,192]{2,1,0:T(8,128)(2,1)} %bitcast.5, f32[1,192]{1,0:T(1,128)} %bitcast.7), custom_call_target="tpu_custom_call" | custom-call | tf_op jit(solution)/shard_map/conv_block/pallas_call | solution.py:252
  19.9 1.7 %copy.7 = bf16[2,4,64,192]{3,2,1,0:T(8,128)(2,1)} copy(bf16[2,4,64,192]{3,2,1,0:T(8,128)(2,1)} %conv_block.1) | data formatting | bytes 393216

commit v3 on v2

--- a/solution.py
+++ b/solution.py
@@ -54,7 +54,6 @@
     out_ref,
     x_ref,
     scales,
-    staged,
     weights,
     packs,
     edges,
@@ -74,7 +73,8 @@
     def at(offsets):
         return {axis: index + offset for axis, index, offset in zip(AXES, position, offsets)}
 
-    around = [(dz, ds, db) for dz in (0, 1) for ds in (-1, 0, 1) for db in (-1, 0, 1) if (dz, ds, db) != (0, 0, 0)]
+    around = [(dz, ds, db) for dz in (0, 1) for ds in (-1, 0, 1) for db in (-1, 0, 1)]
+    around = [o for o in around if o != (0, 0, 0) and (o[0] == 0 or o[1] == 0 or o[2] != 0)]
 
     barrier = pltpu.get_barrier_semaphore()
     for offsets in around:
@@ -98,13 +98,13 @@
     scale_loads = [pltpu.make_async_copy(ref, scales.at[layer], local_sem.at[2 + layer]) for layer, ref in enumerate((s1_hbm, s2_hbm))]
     for copy in scale_loads:
         copy.start()
-    out_copies = [pltpu.make_async_copy(staged.at[frame], out_ref.at[frame], local_sem.at[4 + frame]) for frame in range(2)]
 
     def piece(layer, frame, main, offsets):
         dz, ds, db = offsets
         slot = frame if dz else frames + frame
         if db == 0 and ds == 0:
-            src, dst, kind = main, mains.at[layer, slot], 0
+            part = pl.ds(1, height - 2)
+            src, dst, kind = main.at[part], mains.at[layer, slot, part], 0
         elif db == 0:
             row = height - 1 if ds > 0 else 0
             k = 0 if ds > 0 else 1
@@ -127,10 +127,62 @@
             picked = jnp.concatenate([block[r, column : column + 1] for r in range(height)], axis=0)
             edges[layer, frame, side, 0:height] = picked.astype(jnp.bfloat16)
 
-    def send(layer, frame, main):
-        order = sorted(around, key=lambda o: (o[0], o[2] == 0, o[1] == 0))
-        for offsets in order:
-            guarded(exists(position, sizes, offsets), lambda o=offsets: piece(layer, frame, main, o).start())
+    behind, ahead = exists(position, sizes, (-1, 0, 0)), exists(position, sizes, (1, 0, 0))
+
+    def both(first, second):
+        if first is None or second is None:
+            return None
+        return jnp.logical_and(first, second)
+
+    def edge_row(layer, frame, ds):
+        row, kind = (height - 1, 10) if ds > 0 else (0, 9)
+        return pltpu.make_async_remote_copy(
+            src_ref=packs.at[layer, frame, row],
+            dst_ref=mains.at[layer, frame, row],
+            send_sem=send_sem.at[layer, frame, kind],
+            recv_sem=recv_sem.at[layer, frame, kind],
+            device_id=at((1, 0, 0)),
+            device_id_type=MESH,
+        )
+
+    def passed_on(layer, frame, ds):
+        row, k = (height - 1, 0) if ds > 0 else (0, 1)
+        return pltpu.make_async_remote_copy(
+            src_ref=mains.at[layer, frame, row],
+            dst_ref=rows.at[layer, frame, k],
+            send_sem=send_sem.at[layer, frame, 1 + k],
+            recv_sem=recv_sem.at[layer, frame, 1 + k],
+            device_id=at((0, ds, 0)),
+            device_id_type=MESH,
+        )
+
+    def beside(ds):
+        has = exists(position, sizes, (0, ds, 0))
+        return (None, True) if has is None else (has, jnp.logical_not(has))
+
+    def send_edges(layer, frame, main):
+        for offsets in around:
+            if offsets[0] == 0:
+                guarded(exists(position, sizes, offsets), lambda o=offsets: piece(layer, frame, main, o).start())
+        for ds in (1, -1):
+            guarded(both(ahead, beside(ds)[0]), lambda ds=ds: edge_row(layer, frame, ds).start())
+
+    def send_rest(layer, frame, main):
+        for offsets in around:
+            if offsets[0] == 1 and offsets[2] != 0:
+                guarded(exists(position, sizes, offsets), lambda o=offsets: piece(layer, frame, main, o).start())
+        guarded(ahead, lambda: piece(layer, frame, main, (1, 0, 0)).start())
+        for ds in (1, -1):
+            guarded(both(ahead, beside(ds)[1]), lambda ds=ds: edge_row(layer, frame, ds).start())
+
+    def pass_on(layer, frame):
+        for ds in (1, -1):
+
+            def act(ds=ds):
+                edge_row(layer, frame, ds).wait_recv()
+                passed_on(layer, frame, ds).start()
+
+            guarded(both(behind, beside(ds)[0]), act)
 
     def receive(layer, slot, main):
         dz = 1 if slot < frames else 0
@@ -139,6 +191,10 @@
                 continue
             back = tuple(-o for o in offsets)
             guarded(exists(position, sizes, back), lambda o=offsets: piece(layer, slot % frames, main, o).wait_recv())
+        if dz:
+            for ds in (1, -1):
+                guarded(both(behind, beside(ds)[1]), lambda ds=ds: edge_row(layer, slot, ds).wait_recv())
+                guarded(both(behind, beside(-ds)[0]), lambda ds=ds: passed_on(layer, slot, ds).wait_recv())
 
     def gather(layer, slot, block_ref):
         block = jnp.concatenate([rows[layer, slot, 0][None], block_ref[...], rows[layer, slot, 1][None]], axis=0)
@@ -178,7 +234,9 @@
     pl.semaphore_wait(barrier, count)
 
     for frame in (1, 0):
-        send(0, frame, packs.at[0, frame])
+        send_edges(0, frame, packs.at[0, frame])
+    for frame in (1, 0):
+        send_rest(0, frame, packs.at[0, frame])
 
     def zero(ref, condition):
         def clear():
@@ -206,6 +264,9 @@
         for slot in (3, 2):
             receive(layer, slot, source.at[slot - 2])
             gather(layer, slot, source.at[slot - 2])
+        pass_on(layer, 1)
+        if layer == 0:
+            pass_on(layer, 0)
         loads[layer, 2].wait()
         late = product(layer, 3, 2)
         early = product(layer, 2, 2)
@@ -213,6 +274,8 @@
         late = late + product(layer, 2, 1)
         receive(layer, 1, source.at[1])
         gather(layer, 1, mains.at[layer, 1])
+        if layer == 1:
+            pass_on(layer, 0)
         loads[layer, 0].wait()
         emit(1, finish(late + product(layer, 1, 0), layer))
         early = early + product(layer, 1, 1)
@@ -223,11 +286,11 @@
     def emit_hidden(frame, values):
         packs[1, frame] = pack(values).astype(jnp.bfloat16)
         fill_edges(1, frame, values)
-        send(1, frame, packs.at[1, frame])
+        send_edges(1, frame, packs.at[1, frame])
+        send_rest(1, frame, packs.at[1, frame])
 
     def emit_output(frame, values):
-        staged[frame] = values.astype(jnp.bfloat16)
-        out_copies[frame].start()
+        out_ref[frame] = values.astype(jnp.bfloat16)
 
     conv_layer(0, packs.at[0], emit_hidden)
     conv_layer(1, packs.at[1], emit_output)
@@ -239,8 +302,9 @@
                     exists(position, sizes, offsets),
                     lambda o=offsets: piece(layer, frame, packs.at[layer, frame], o).wait_send(),
                 )
-    for copy in out_copies:
-        copy.wait()
+            for ds in (1, -1):
+                guarded(ahead, lambda ds=ds: edge_row(layer, frame, ds).wait_send())
+                guarded(both(behind, beside(ds)[0]), lambda ds=ds: passed_on(layer, frame, ds).wait_send())
 
 
 def shards(sizes, frames_in, weight_first, scale_first, weight_second, scale_second):
@@ -251,13 +315,12 @@
     half = jnp.bfloat16
     return pl.pallas_call(
         functools.partial(kernel, sizes),
-        out_shape=jax.ShapeDtypeStruct(frames_in.shape, half),
+        out_shape=pltpu.VMEM(frames_in.shape, half),
         in_specs=[anywhere] * 5,
-        out_specs=anywhere,
+        out_specs=pl.BlockSpec(memory_space=pltpu.VMEM),
         scratch_shapes=[
             pltpu.VMEM(frames_in.shape, half),
             pltpu.VMEM((2, 1, channels), jnp.float32),
-            pltpu.VMEM(frames_in.shape, half),
             pltpu.VMEM((2, *flat), half),
             pltpu.VMEM((2, frames, height, lines, 128), half),
             pltpu.VMEM((2, frames, 2, 8, channels), half),
@@ -265,10 +328,10 @@
             pltpu.VMEM((2, 2 * frames, 2, lines, 128), half),
             pltpu.VMEM((2, 2 * frames, 3, 2, 8, channels), half),
             pltpu.VMEM((2 * frames, height * width, 9 * channels), half),
-            pltpu.SemaphoreType.DMA((6,)),
+            pltpu.SemaphoreType.DMA((4,)),
             pltpu.SemaphoreType.DMA((2, 3)),
-            pltpu.SemaphoreType.DMA((2, 2 * frames, 9)),
-            pltpu.SemaphoreType.DMA((2, 2 * frames, 9)),
+            pltpu.SemaphoreType.DMA((2, 2 * frames, 11)),
+            pltpu.SemaphoreType.DMA((2, 2 * frames, 11)),
         ],
         compiler_params=pltpu.CompilerParams(collective_id=0, has_side_effects=True),
         name="conv_block",

time: 21.7 us -> 23.8 us (1.097)
  the two profiles are of different devices: /device:TPU:0 before, /device:TPU:16 now
where the time goes in v3:
time: 23.8 us; the launch traced here: 23.7 us
  Pallas kernels  23 us (97%)
  local copies, waits for them, and re-layouts  0.71 us (3%)
    pallas_call x1, Pallas kernels, shards(): pl.pallas_call(functools.partial(kernel, sizes), out_shape=pltpu.VMEM(fra...  23 us
    unnamed x1, local copies, waits for them, and re-layouts  0.71 us

profile of v3, /device:TPU:16, one launch (start us, length us, event | category | flops | bytes accessed | tf_op | source)
XLA Modules:
  0.0 23.7 jit_solution(10385217854041453469)
XLA Ops:
  0.0 23.0 %conv_block.1 = bf16[2,4,64,192]{3,2,1,0:T(8,128)(2,1)S(1)} custom-call(bf16[2,4,64,192]{3,2,1,0:T(8,128)(2,1)} %x_hbm.1, bf16[3,1728,192]{2,1,0:T(8,128)(2,1)} %bitcast.4, f32[1,192]{1,0:T(1,128)} %bitcast.6, bf16[3,1728,192]{2,1,0:T(8,128)(2,1)} %bitcast.5, f32[1,192]{1,0:T(1,128)} %bitcast.7), custom_call_target="tpu_custom_call" | custom-call | tf_op jit(solution)/shard_map/conv_block/pallas_call | solution.py:316
  23.0 0.7 %copy.7 = bf16[2,4,64,192]{3,2,1,0:T(8,128)(2,1)} copy(bf16[2,4,64,192]{3,2,1,0:T(8,128)(2,1)S(1)} %conv_block.1) | data formatting | bytes 393216

commit v4 on v2

--- a/solution.py
+++ b/solution.py
@@ -54,7 +54,6 @@
     out_ref,
     x_ref,
     scales,
-    staged,
     weights,
     packs,
     edges,
@@ -98,7 +97,6 @@
     scale_loads = [pltpu.make_async_copy(ref, scales.at[layer], local_sem.at[2 + layer]) for layer, ref in enumerate((s1_hbm, s2_hbm))]
     for copy in scale_loads:
         copy.start()
-    out_copies = [pltpu.make_async_copy(staged.at[frame], out_ref.at[frame], local_sem.at[4 + frame]) for frame in range(2)]
 
     def piece(layer, frame, main, offsets):
         dz, ds, db = offsets
@@ -203,11 +201,12 @@
         copy.wait()
 
     def conv_layer(layer, source, emit):
-        for slot in (3, 2):
-            receive(layer, slot, source.at[slot - 2])
-            gather(layer, slot, source.at[slot - 2])
+        receive(layer, 3, source.at[1])
+        gather(layer, 3, source.at[1])
         loads[layer, 2].wait()
         late = product(layer, 3, 2)
+        receive(layer, 2, source.at[0])
+        gather(layer, 2, source.at[0])
         early = product(layer, 2, 2)
         loads[layer, 1].wait()
         late = late + product(layer, 2, 1)
@@ -226,8 +225,7 @@
         send(1, frame, packs.at[1, frame])
 
     def emit_output(frame, values):
-        staged[frame] = values.astype(jnp.bfloat16)
-        out_copies[frame].start()
+        out_ref[frame] = values.astype(jnp.bfloat16)
 
     conv_layer(0, packs.at[0], emit_hidden)
     conv_layer(1, packs.at[1], emit_output)
@@ -239,8 +237,6 @@
                     exists(position, sizes, offsets),
                     lambda o=offsets: piece(layer, frame, packs.at[layer, frame], o).wait_send(),
                 )
-    for copy in out_copies:
-        copy.wait()
 
 
 def shards(sizes, frames_in, weight_first, scale_first, weight_second, scale_second):
@@ -251,13 +247,12 @@
     half = jnp.bfloat16
     return pl.pallas_call(
         functools.partial(kernel, sizes),
-        out_shape=jax.ShapeDtypeStruct(frames_in.shape, half),
+        out_shape=pltpu.VMEM(frames_in.shape, half),
         in_specs=[anywhere] * 5,
-        out_specs=anywhere,
+        out_specs=pl.BlockSpec(memory_space=pltpu.VMEM),
         scratch_shapes=[
             pltpu.VMEM(frames_in.shape, half),
             pltpu.VMEM((2, 1, channels), jnp.float32),
-            pltpu.VMEM(frames_in.shape, half),
             pltpu.VMEM((2, *flat), half),
             pltpu.VMEM((2, frames, height, lines, 128), half),
             pltpu.VMEM((2, frames, 2, 8, channels), half),
@@ -265,7 +260,7 @@
             pltpu.VMEM((2, 2 * frames, 2, lines, 128), half),
             pltpu.VMEM((2, 2 * frames, 3, 2, 8, channels), half),
             pltpu.VMEM((2 * frames, height * width, 9 * channels), half),
-            pltpu.SemaphoreType.DMA((6,)),
+            pltpu.SemaphoreType.DMA((4,)),
             pltpu.SemaphoreType.DMA((2, 3)),
             pltpu.SemaphoreType.DMA((2, 2 * frames, 9)),
             pltpu.SemaphoreType.DMA((2, 2 * frames, 9)),

time: 21.7 us -> 20 us (0.922)
  local copies, waits for them, and re-layouts: 1.67 us -> 0.71 us
  Pallas kernels: 19.9 us -> 19.1 us
    unnamed x1, local copies, waits for them, and re-layouts: 1.67 us -> 0.71 us
    pallas_call x1, Pallas kernels: 19.9 us -> 19.1 us  [shards(): pl.pallas_call(functools.partial(kernel, sizes), out_shape=pltpu.VMEM(fra...]
where the time goes in v4:
time: 20 us; the launch traced here: 19.9 us
  Pallas kernels  19.1 us (96%)
  local copies, waits for them, and re-layouts  0.71 us (4%)
    pallas_call x1, Pallas kernels, shards(): pl.pallas_call(functools.partial(kernel, sizes), out_shape=pltpu.VMEM(fra...  19.1 us
    unnamed x1, local copies, waits for them, and re-layouts  0.71 us

profile of v4, /device:TPU:0, one launch (start us, length us, event | category | flops | bytes accessed | tf_op | source)
XLA Modules:
  0.0 19.9 jit_solution(4665818190106015582)
XLA Ops:
  0.0 19.1 %conv_block.1 = bf16[2,4,64,192]{3,2,1,0:T(8,128)(2,1)S(1)} custom-call(bf16[2,4,64,192]{3,2,1,0:T(8,128)(2,1)} %x_hbm.1, bf16[3,1728,192]{2,1,0:T(8,128)(2,1)} %bitcast.4, f32[1,192]{1,0:T(1,128)} %bitcast.6, bf16[3,1728,192]{2,1,0:T(8,128)(2,1)} %bitcast.5, f32[1,192]{1,0:T(1,128)} %bitcast.7), custom_call_target="tpu_custom_call" | custom-call | tf_op jit(solution)/shard_map/conv_block/pallas_call | solution.py:248
  19.1 0.7 %copy.7 = bf16[2,4,64,192]{3,2,1,0:T(8,128)(2,1)} copy(bf16[2,4,64,192]{3,2,1,0:T(8,128)(2,1)S(1)} %conv_block.1) | data formatting | bytes 393216

commit v5 on v4

--- a/solution.py
+++ b/solution.py
@@ -205,19 +205,30 @@
         gather(layer, 3, source.at[1])
         loads[layer, 2].wait()
         late = product(layer, 3, 2)
-        receive(layer, 2, source.at[0])
-        gather(layer, 2, source.at[0])
-        early = product(layer, 2, 2)
-        loads[layer, 1].wait()
-        late = late + product(layer, 2, 1)
-        receive(layer, 1, source.at[1])
-        gather(layer, 1, mains.at[layer, 1])
-        loads[layer, 0].wait()
-        emit(1, finish(late + product(layer, 1, 0), layer))
-        early = early + product(layer, 1, 1)
-        receive(layer, 0, source.at[0])
-        gather(layer, 0, mains.at[layer, 0])
-        emit(0, finish(early + product(layer, 0, 0), layer))
+        own = lambda: (receive(layer, 2, source.at[0]), gather(layer, 2, source.at[0]))
+        got = lambda slot: (receive(layer, slot, source.at[slot]), gather(layer, slot, mains.at[layer, slot]))
+        if layer == 0:
+            own()
+            early = product(layer, 2, 2)
+            loads[layer, 1].wait()
+            late = late + product(layer, 2, 1)
+            got(1)
+            loads[layer, 0].wait()
+            emit(1, finish(late + product(layer, 1, 0), layer))
+            early = early + product(layer, 1, 1)
+            got(0)
+            emit(0, finish(early + product(layer, 0, 0), layer))
+        else:
+            got(1)
+            loads[layer, 0].wait()
+            late = late + product(layer, 1, 0)
+            loads[layer, 1].wait()
+            early = product(layer, 1, 1)
+            own()
+            early = early + product(layer, 2, 2)
+            emit(1, finish(late + product(layer, 2, 1), layer))
+            got(0)
+            emit(0, finish(early + product(layer, 0, 0), layer))
 
     def emit_hidden(frame, values):
         packs[1, frame] = pack(values).astype(jnp.bfloat16)

time: 20 us -> 18.7 us (0.935)
  Pallas kernels: 19.1 us -> 17.6 us
    pallas_call x1, Pallas kernels: 19.1 us -> 17.6 us  [shards(): pl.pallas_call(functools.partial(kernel, sizes), out_shape=pltpu.VMEM(fra...]
where the time goes in v5:
time: 18.7 us; the launch traced here: 18.4 us
  Pallas kernels  17.6 us (94%)
  local copies, waits for them, and re-layouts  0.71 us (4%)
    pallas_call x1, Pallas kernels, shards(): pl.pallas_call(functools.partial(kernel, sizes), out_shape=pltpu.VMEM(fra...  17.6 us
    unnamed x1, local copies, waits for them, and re-layouts  0.71 us

profile of v5, /device:TPU:0, one launch (start us, length us, event | category | flops | bytes accessed | tf_op | source)
XLA Modules:
  0.0 18.4 jit_solution(5036212060691668132)
XLA Ops:
  0.0 17.6 %conv_block.1 = bf16[2,4,64,192]{3,2,1,0:T(8,128)(2,1)S(1)} custom-call(bf16[2,4,64,192]{3,2,1,0:T(8,128)(2,1)} %x_hbm.1, bf16[3,1728,192]{2,1,0:T(8,128)(2,1)} %bitcast.4, f32[1,192]{1,0:T(1,128)} %bitcast.6, bf16[3,1728,192]{2,1,0:T(8,128)(2,1)} %bitcast.5, f32[1,192]{1,0:T(1,128)} %bitcast.7), custom_call_target="tpu_custom_call" | custom-call | tf_op jit(solution)/shard_map/conv_block/pallas_call | solution.py:259
  17.7 0.7 %copy.7 = bf16[2,4,64,192]{3,2,1,0:T(8,128)(2,1)} copy(bf16[2,4,64,192]{3,2,1,0:T(8,128)(2,1)S(1)} %conv_block.1) | data formatting | bytes 393216
